TPU v7x, 32 devices: a whole 2x2x4 slice. The times are simulated.
32 devices in a mesh: dp: 16 (over z, y, x), mp: 2 (over core).
Axes of the slice: x: 2, y: 2, z: 4, core: 2. Of those that a mesh axis runs over, the one named last changes fastest.
Arguments:
- tokens: bfloat16 [32, 512, 768], P('dp', 'mp'), may hold values from -6 to 6
- lengths: int32 [32, 16], P('dp'), may hold values from 0 to 512, as said below
- cotangent: bfloat16 [32, 512, 768], P('dp', 'mp'), may hold values from -6 to 6
- w_query: bfloat16 [2, 768, 768], P(None, None, 'mp'), may hold values from -0.21875 to 0.21875
- b_query: bfloat16 [2, 768], P(None, 'mp'), may hold values from -3 to 3
- w_key: bfloat16 [2, 768, 768], P(None, None, 'mp'), may hold values from -0.21875 to 0.21875
- w_value: bfloat16 [2, 768, 768], P(None, None, 'mp'), may hold values from -0.21875 to 0.21875
- b_value: bfloat16 [2, 768], P(None, 'mp'), may hold values from -3 to 3
- w_out: bfloat16 [2, 768, 768], P(None, None, 'mp'), may hold values from -1.75 to 1.75
- b_out: bfloat16 [2, 768], replicated, may hold values from -3 to 3
- first_gain: bfloat16 [2, 768], replicated, may hold values from 0.099609375 to 1.8984375
- first_shift: bfloat16 [2, 768], replicated, may hold values from -3 to 3
- w_up: bfloat16 [2, 768, 3072], P(None, None, 'mp'), may hold values from -0.21875 to 0.21875
- b_up: bfloat16 [2, 3072], P(None, 'mp'), may hold values from -3 to 3
- w_down: bfloat16 [2, 768, 3072], P(None, None, 'mp'), may hold values from -0.109375 to 0.109375
- b_down: bfloat16 [2, 768], replicated, may hold values from -3 to 3
- second_gain: bfloat16 [2, 768], replicated, may hold values from 0.099609375 to 1.8984375
- second_shift: bfloat16 [2, 768], replicated, may hold values from -3 to 3
Outputs:
- encoded: bfloat16 [32, 512, 768], P('dp', 'mp')
- token_grad: float32 [32, 512, 768], P('dp', 'mp')
- grad_w_query: float32 [2, 768, 768], P(None, 'dp', 'mp')
- grad_b_query: float32 [2, 768], P(None, 'mp')
- grad_w_key: float32 [2, 768, 768], P(None, 'dp', 'mp')
- grad_w_value: float32 [2, 768, 768], P(None, 'dp', 'mp')
- grad_b_value: float32 [2, 768], P(None, 'mp')
- grad_w_out: float32 [2, 768, 768], P(None, 'dp', 'mp')
- grad_b_out: float32 [2, 768], replicated
- grad_first_gain: float32 [2, 768], replicated
- grad_first_shift: float32 [2, 768], replicated
- grad_w_up: float32 [2, 768, 3072], P(None, 'dp', 'mp')
- grad_b_up: float32 [2, 3072], P(None, 'mp')
- grad_w_down: float32 [2, 768, 3072], P(None, 'dp', 'mp')
- grad_b_down: float32 [2, 768], replicated
- grad_second_gain: float32 [2, 768], replicated
- grad_second_shift: float32 [2, 768], replicated
Inputs may be any that keep to these rules, and one draw needn't show every extreme that they name: In each row either entries 1 to 15 are 0 and entry 0 is a passage's length, at least 64, or all 16 entries are lengths of queries, each at least 1 and at most 32. Some row holds a passage of 512 slots and some query fills its 32 slots.
All inputs are finite; a program needn't handle non-finite values.
Results may differ from a plain program's by a relative error of at most 0.04.
Values may be sent and summed in bfloat16 or wider, within the bound.
No kernel may reach another device: no remote copies, remote signals or barrier semaphores. Data moves between devices by JAX's collectives and lax.ppermute only.
A program may use at most 192 MiB of HBM per device.

v0:
```python
import jax
import jax.numpy as jnp
from jax import lax
from jax.sharding import PartitionSpec as P

DH = 64
SLOTS = 512
QSLOT = 32
SEGS = 16


def visible_mask(lengths):
    slot_index = jnp.arange(SLOTS, dtype=jnp.int32)
    is_query = lengths[:, 1] > 0
    segment_width = jnp.where(is_query, QSLOT, SLOTS).astype(jnp.int32)[:, None]
    segment = slot_index[None, :] // segment_width
    inside = slot_index[None, :] - segment * segment_width
    onehot = segment[:, :, None] == jnp.arange(SEGS, dtype=jnp.int32)[None, None, :]
    segment_length = jnp.sum(jnp.where(onehot, lengths[:, None, :], 0), axis=2)
    live_keys = inside < segment_length
    same_segment = segment[:, :, None] == segment[:, None, :]
    return same_segment & live_keys[:, None, :]


def layer_norm(residual, norm_gain, norm_shift):
    average = jnp.mean(residual, axis=-1, keepdims=True)
    centred = residual - average
    variance = jnp.mean(centred * centred, axis=-1, keepdims=True)
    return centred * lax.rsqrt(variance + 1e-12) * norm_gain + norm_shift


def gelu_exact(argument):
    return 0.5 * argument * (1.0 + jax.scipy.special.erf(argument * 0.7071067811865476))


def project(left, right):
    return jnp.einsum("rsd,de->rse", left, right, preferred_element_type=jnp.float32)


def attend(row_data):
    row_queries, row_keys, row_values, visible = row_data
    head_count = row_queries.shape[1] // DH
    query_heads = row_queries.reshape(SLOTS, head_count, DH)
    key_heads = row_keys.reshape(SLOTS, head_count, DH)
    value_heads = row_values.reshape(SLOTS, head_count, DH)
    scores = jnp.einsum(
        "shd,thd->hst", query_heads, key_heads, preferred_element_type=jnp.float32
    ) * DH ** (-0.5)
    scores = jnp.where(visible[None], scores, -1000000000.0)
    row_peak = jnp.max(scores, axis=2, keepdims=True)
    exponent = jnp.exp(scores - row_peak)
    summed = jnp.sum(exponent, axis=2, keepdims=True)
    weights_low = (exponent / summed).astype(jnp.bfloat16)
    context = jnp.einsum(
        "hst,thd->shd", weights_low, value_heads, preferred_element_type=jnp.float32
    )
    return (
        context.reshape(SLOTS, head_count * DH).astype(jnp.bfloat16),
        (row_peak + jnp.log(summed))[:, :, 0],
    )


def attend_back(row_data):
    row_queries, row_keys, row_values, visible, log_total, context_grad = row_data
    head_count = row_queries.shape[1] // DH
    width = head_count * DH
    query_heads = row_queries.reshape(SLOTS, head_count, DH)
    key_heads = row_keys.reshape(SLOTS, head_count, DH)
    value_heads = row_values.reshape(SLOTS, head_count, DH)
    grad_heads = context_grad.reshape(SLOTS, head_count, DH)
    scores = jnp.einsum(
        "shd,thd->hst", query_heads, key_heads, preferred_element_type=jnp.float32
    ) * DH ** (-0.5)
    probabilities = jnp.where(visible[None], jnp.exp(scores - log_total[:, :, None]), 0.0)
    weights_low = probabilities.astype(jnp.bfloat16)
    value_grad = jnp.einsum(
        "hst,shd->thd", weights_low, grad_heads, preferred_element_type=jnp.float32
    )
    weight_grad = jnp.einsum(
        "shd,thd->hst", grad_heads, value_heads, preferred_element_type=jnp.float32
    )
    score_grad = (
        probabilities * (weight_grad - jnp.sum(probabilities * weight_grad, axis=2, keepdims=True))
    ).astype(jnp.bfloat16)
    query_grad = jnp.einsum(
        "hst,thd->shd", score_grad, key_heads, preferred_element_type=jnp.float32
    ) * DH ** (-0.5)
    key_grad = jnp.einsum(
        "hst,shd->thd", score_grad, query_heads, preferred_element_type=jnp.float32
    ) * DH ** (-0.5)
    return (
        query_grad.reshape(SLOTS, width).astype(jnp.bfloat16),
        key_grad.reshape(SLOTS, width).astype(jnp.bfloat16),
        value_grad.reshape(SLOTS, width).astype(jnp.bfloat16),
    )


def forward_layer(block_in, weights, visibility):
    (
        w_query,
        b_query,
        w_key,
        w_value,
        b_value,
        w_out,
        b_out,
        first_gain,
        first_shift,
        w_up,
        b_up,
        w_down,
        b_down,
        second_gain,
        second_shift,
    ) = weights
    gathered = lax.all_gather(block_in, "mp", axis=1, tiled=True)
    queries = (project(gathered, w_query) + b_query.astype(jnp.float32)).astype(jnp.bfloat16)
    keys_all = project(gathered, w_key).astype(jnp.bfloat16)
    values_all = (project(gathered, w_value) + b_value.astype(jnp.float32)).astype(jnp.bfloat16)
    context, log_total = lax.map(attend, (queries, keys_all, values_all, visibility))
    partial_out = jnp.einsum("rsc,dc->rsd", context, w_out, preferred_element_type=jnp.float32)
    attended = lax.psum_scatter(
        partial_out.astype(jnp.bfloat16), "mp", scatter_dimension=1, tiled=True
    ).astype(jnp.float32) + b_out.astype(jnp.float32)
    first_resid = block_in.astype(jnp.float32) + attended
    normed = layer_norm(
        first_resid, first_gain.astype(jnp.float32), first_shift.astype(jnp.float32)
    )
    gathered_normed = lax.all_gather(normed.astype(jnp.bfloat16), "mp", axis=1, tiled=True)
    upward = project(gathered_normed, w_up) + b_up.astype(jnp.float32)
    activated = gelu_exact(upward).astype(jnp.bfloat16)
    partial_down = jnp.einsum("rsf,df->rsd", activated, w_down, preferred_element_type=jnp.float32)
    downward = lax.psum_scatter(
        partial_down.astype(jnp.bfloat16), "mp", scatter_dimension=1, tiled=True
    ).astype(jnp.float32) + b_down.astype(jnp.float32)
    second_resid = normed + downward
    output = layer_norm(
        second_resid, second_gain.astype(jnp.float32), second_shift.astype(jnp.float32)
    )
    kept_state = (
        gathered,
        queries,
        keys_all,
        values_all,
        context,
        log_total,
        first_resid,
        gathered_normed,
        upward,
        activated,
        second_resid,
    )
    return (output, kept_state)


def backward_layer(weights, visibility, kept_state, grad_out):
    (
        w_query,
        b_query,
        w_key,
        w_value,
        b_value,
        w_out,
        b_out,
        first_gain,
        first_shift,
        w_up,
        b_up,
        w_down,
        b_down,
        second_gain,
        second_shift,
    ) = weights
    (
        gathered,
        queries,
        keys_all,
        values_all,
        context,
        log_total,
        first_resid,
        gathered_normed,
        upward,
        activated,
        second_resid,
    ) = kept_state
    unused, pull_second = jax.vjp(
        layer_norm, second_resid, second_gain.astype(jnp.float32), second_shift.astype(jnp.float32)
    )
    grad_second, grad_second_gain, grad_second_shift = pull_second(grad_out)
    down_grad = grad_second.astype(jnp.bfloat16)
    grad_b_down = jnp.sum(down_grad, axis=(0, 1), dtype=jnp.float32)
    gathered_down = lax.all_gather(down_grad, "mp", axis=1, tiled=True)
    grad_w_down = jnp.einsum(
        "rsd,rsf->df", gathered_down, activated, preferred_element_type=jnp.float32
    )
    act_grad = jnp.einsum("rsd,df->rsf", gathered_down, w_down, preferred_element_type=jnp.float32)
    unused, pull_gelu = jax.vjp(gelu_exact, upward)
    up_grad = pull_gelu(act_grad)[0].astype(jnp.bfloat16)
    grad_b_up = jnp.sum(up_grad, axis=(0, 1), dtype=jnp.float32)
    grad_w_up = jnp.einsum(
        "rsd,rsf->df", gathered_normed, up_grad, preferred_element_type=jnp.float32
    )
    partial_normed = jnp.einsum("rsf,df->rsd", up_grad, w_up, preferred_element_type=jnp.float32)
    normed_grad = grad_second + lax.psum_scatter(
        partial_normed.astype(jnp.bfloat16), "mp", scatter_dimension=1, tiled=True
    ).astype(jnp.float32)
    unused, pull_first = jax.vjp(
        layer_norm, first_resid, first_gain.astype(jnp.float32), first_shift.astype(jnp.float32)
    )
    grad_first, grad_first_gain, grad_first_shift = pull_first(normed_grad)
    out_grad = grad_first.astype(jnp.bfloat16)
    grad_b_out = jnp.sum(out_grad, axis=(0, 1), dtype=jnp.float32)
    gathered_out = lax.all_gather(out_grad, "mp", axis=1, tiled=True)
    grad_w_out = jnp.einsum(
        "rsd,rsc->dc", gathered_out, context, preferred_element_type=jnp.float32
    )
    context_grad = jnp.einsum(
        "rsd,dc->rsc", gathered_out, w_out, preferred_element_type=jnp.float32
    ).astype(jnp.bfloat16)
    query_grad, key_grad, value_grad = lax.map(
        attend_back, (queries, keys_all, values_all, visibility, log_total, context_grad)
    )
    grad_b_query = jnp.sum(query_grad, axis=(0, 1), dtype=jnp.float32)
    grad_b_value = jnp.sum(value_grad, axis=(0, 1), dtype=jnp.float32)
    grad_w_query = jnp.einsum(
        "rsd,rse->de", gathered, query_grad, preferred_element_type=jnp.float32
    )
    grad_w_key = jnp.einsum("rsd,rse->de", gathered, key_grad, preferred_element_type=jnp.float32)
    grad_w_value = jnp.einsum(
        "rsd,rse->de", gathered, value_grad, preferred_element_type=jnp.float32
    )
    partial_in = jnp.einsum("rse,de->rsd", query_grad, w_query, preferred_element_type=jnp.float32)
    partial_in = partial_in + jnp.einsum(
        "rse,de->rsd", key_grad, w_key, preferred_element_type=jnp.float32
    )
    partial_in = partial_in + jnp.einsum(
        "rse,de->rsd", value_grad, w_value, preferred_element_type=jnp.float32
    )
    block_grad = grad_first + lax.psum_scatter(
        partial_in.astype(jnp.bfloat16), "mp", scatter_dimension=1, tiled=True
    ).astype(jnp.float32)
    gradients = (
        grad_w_query,
        grad_b_query,
        grad_w_key,
        grad_w_value,
        grad_b_value,
        grad_w_out,
        grad_b_out,
        grad_first_gain,
        grad_first_shift,
        grad_w_up,
        grad_b_up,
        grad_w_down,
        grad_b_down,
        grad_second_gain,
        grad_second_shift,
    )
    return (block_grad, gradients)


def shards(
    tokens,
    lengths,
    cotangent,
    w_query,
    b_query,
    w_key,
    w_value,
    b_value,
    w_out,
    b_out,
    first_gain,
    first_shift,
    w_up,
    b_up,
    w_down,
    b_down,
    second_gain,
    second_shift,
):
    params = (
        w_query,
        b_query,
        w_key,
        w_value,
        b_value,
        w_out,
        b_out,
        first_gain,
        first_shift,
        w_up,
        b_up,
        w_down,
        b_down,
        second_gain,
        second_shift,
    )
    visibility = visible_mask(lengths)
    layer_count = w_query.shape[0]
    block_inputs = []
    kept_states = []
    hidden = tokens
    for layer_index in range(layer_count):
        weights = tuple((member[layer_index] for member in params))
        block_inputs.append(hidden)
        output, kept_state = forward_layer(hidden, weights, visibility)
        kept_states.append(kept_state)
        hidden = output.astype(jnp.bfloat16)
    grad_hidden = cotangent.astype(jnp.float32)
    layer_grads = [None] * layer_count
    for layer_index in reversed(range(layer_count)):
        weights = tuple((member[layer_index] for member in params))
        kept_state = forward_layer(block_inputs[layer_index], weights, visibility)[1]
        grad_hidden, gradients = backward_layer(weights, visibility, kept_state, grad_hidden)
        layer_grads[layer_index] = gradients
    stacked = [
        jnp.stack([layer_grads[layer_index][member_index] for layer_index in range(layer_count)])
        for member_index in range(15)
    ]
    matrices = (
        lax.psum_scatter(stacked[0], "dp", scatter_dimension=1, tiled=True),
        lax.psum_scatter(stacked[2], "dp", scatter_dimension=1, tiled=True),
        lax.psum_scatter(stacked[3], "dp", scatter_dimension=1, tiled=True),
        lax.psum_scatter(stacked[5], "dp", scatter_dimension=1, tiled=True),
        lax.psum_scatter(stacked[9], "dp", scatter_dimension=1, tiled=True),
        lax.psum_scatter(stacked[11], "dp", scatter_dimension=1, tiled=True),
    )
    columns = lax.psum((stacked[1], stacked[4], stacked[10]), "dp")
    rows_summed = lax.psum(
        (stacked[6], stacked[7], stacked[8], stacked[12], stacked[13], stacked[14]), ("dp", "mp")
    )
    return (
        hidden,
        grad_hidden,
        matrices[0],
        columns[0],
        matrices[1],
        matrices[2],
        columns[1],
        matrices[3],
        rows_summed[0],
        rows_summed[1],
        rows_summed[2],
        matrices[4],
        columns[2],
        matrices[5],
        rows_summed[3],
        rows_summed[4],
        rows_summed[5],
    )


def solution(mesh):
    placed = (
        P("dp", "mp", None),
        P("dp", None),
        P("dp", "mp", None),
        P(None, None, "mp"),
        P(None, "mp"),
        P(None, None, "mp"),
        P(None, None, "mp"),
        P(None, "mp"),
        P(None, None, "mp"),
        P(),
        P(),
        P(),
        P(None, None, "mp"),
        P(None, "mp"),
        P(None, None, "mp"),
        P(),
        P(),
        P(),
    )
    return jax.shard_map(
        shards,
        mesh=mesh,
        in_specs=placed,
        out_specs=(
            P("dp", "mp", None),
            P("dp", "mp", None),
            P(None, "dp", "mp"),
            P(None, "mp"),
            P(None, "dp", "mp"),
            P(None, "dp", "mp"),
            P(None, "mp"),
            P(None, "dp", "mp"),
            P(),
            P(),
            P(),
            P(None, "dp", "mp"),
            P(None, "mp"),
            P(None, "dp", "mp"),
            P(),
            P(),
            P(),
        ),
        check_vma=False,
    )
```

profile of v0, /device:TPU:0, one launch (start us, length us, event | category | flops | bytes accessed | tf_op | source)
XLA Modules:
  0.0 1289.5 jit_solution(6457793700679230937)
XLA Ops:
  13.4 8.7 all-gather.11.cloned.1.call-done
  37.4 24.5 %while.72 = (s32[]{:T(128)}, bf16[2,512,384]{1,2,0:T(8,128)(2,1)}, bf16[2,512,384]{1,2,0:T(8,128)(2,1)S(1)}, pred[2,512,512]{1,2,0:T(8,128)(4,1)S(1)}, bf16[2,51...) while((s32[]{:T(128)}, bf16[2,512,384]{1,2,0:T(8,128)(2,1)}, ...), condition=%wide.region_4.5_spmd, body=%wide.region_1.4_spmd.sunk | while | flops 412287488 | bytes 24404124 | solution.py:120
  66.9 11.2 while.76
  97.7 10.5 all-gather.13.cloned.1.call-done
  108.1 9.2 fusion.93
  118.6 9.1 reduce-scatter.18.cloned.1.call-done
  132.6 11.1 all-gather.25.cloned.1.call-done
  158.6 9.1 reduce-scatter.34.cloned.1.call-done
  172.7 11.1 all-gather.15.cloned.1.call-done
  198.1 22.5 %while.73 = (s32[]{:T(128)}, bf16[2,512,384]{1,2,0:T(8,128)(2,1)}, bf16[2,512,384]{1,2,0:T(8,128)(2,1)S(1)}, pred[2,512,512]{1,2,0:T(8,128)(4,1)S(1)}, bf16[2,51...) while((s32[]{:T(128)}, bf16[2,512,384]{1,2,0:T(8,128)(2,1)}, ...), condition=%wide.region_14.15_spmd, body=%wide.region_11.14_spmd.sunk | while | flops 412287488 | bytes 24404124 | solution.py:120
  224.7 11.4 while.74
  242.3 8.7 reduce-scatter.24.cloned.1.call-done
  254.5 11.1 all-gather.17.cloned.1.call-done
  265.6 9.2 fusion.102
  275.1 10.2 reduce-scatter.22.cloned.1.call-done
  289.3 11.1 all-gather.19.cloned.1.call-done
  314.1 10.3 reduce-scatter.26.cloned.1.call-done
  332.3 11.1 all-gather.21.cloned.1.call-done
  358.6 10.3 reduce-scatter.28.cloned.1.call-done
  377.2 10.9 all-gather.23.cloned.1.call-done
  393.5 30.1 %while.75 = (s32[]{:T(128)}, bf16[2,512,384]{1,2,0:T(8,128)(2,1)}, bf16[2,512,384]{1,2,0:T(8,128)(2,1)}, bf16[2,512,384]{1,2,0:T(8,128)(2,1)}, bf16[2,512,384]{1...) while((s32[]{:T(128)}, bf16[2,512,384]{1,2,0:T(8,128)(2,1)}, ...), condition=%wide.region_38.39_spmd, body=%wide.region_36.38_spmd.sunk | while | flops 1031205888 | bytes 93606456 | solution.py:221
  431.6 8.7 reduce-scatter.30.cloned.1.call-done
  447.4 11.1 all-gather.27.cloned.1.call-done
  472.3 10.3 reduce-scatter.36.cloned.1.call-done
  488.9 11.0 all-gather.29.cloned.1.call-done
  505.1 32.2 %while.77 = (s32[]{:T(128)}, bf16[2,512,384]{1,2,0:T(8,128)(2,1)}, bf16[2,512,384]{1,2,0:T(8,128)(2,1)}, bf16[2,512,384]{1,2,0:T(8,128)(2,1)}, bf16[2,512,384]{1...) while((s32[]{:T(128)}, bf16[2,512,384]{1,2,0:T(8,128)(2,1)}, ...), condition=%wide.region_57.58_spmd, body=%wide.region_55.57_spmd.sunk | while | flops 1031205888 | bytes 87118264 | solution.py:221
  605.9 43.8 %all-reduce.3 = (f32[2,768]{1,0:T(2,128)}, f32[2,768]{1,0:T(2,128)}, f32[2,768]{1,0:T(2,128)}, f32[2,768]{1,0:T(2,128)}, f32[2,768]{1,0:T(2,128)}, /*index=5*/f32[2,768]{1,0:T(2,128)}) all-reduce(f32[2,768]{1,0:T(2,128)S(1)} %pad_maximum_fusion.7, f32[2,768]{1,0:T(2,128)S(1)} %pad_maximum_fusion.8, ...), channel_id=1, replica_groups=mesh['dp'=16,'mp'=2] {'dp','mp'}, use_global_device_ids=true, to_apply=%region_71.72 | all-reduce | flops 9216 | bytes 73728 | tf_op jit(solution)/shard_map/psum | solution.py:331
  650.2 76.6 %all-reduce.4 = (f32[2,384]{1,0:T(2,128)}, f32[2,384]{1,0:T(2,128)}, f32[2,1536]{1,0:T(2,128)}) all-reduce(f32[2,384]{1,0:T(2,128)S(1)} %pad_maximum_fusion.13, f32[2,384]{1,0:T(2,128)S(1)} %pad_maximum_fusion.14, f32[2,1536]{1,0:T(2,128)S(1)} %pad_maximum_fusion.6), channel_id=1, replica_groups=mesh['dp'=16,'mp'=2] {'dp'}, use_global_device_ids=true, to_apply=%region_62.63 | all-reduce | flops 4608 | bytes 36864 | tf_op jit(solution)/shard_map/psum | solution.py:330
  729.2 68.2 %all-reduce.8.cloned.1.call-done = (f32[2,768,384]{2,0,1:T(2,128)}, f32[2,768,384]{2,0,1:T(2,128)}, f32[2,768,384]{2,0,1:T(2,128)}) async-done(((f32[2,768,384]{2,0,1:T(2,128)}, f32[2,768,384]{2,0,1:T(2,128)}, f32[2,768,384]{2,0,1:T(2,128)}), (f32[2,768,384]{2,0,1:T(2,128)}, f32[2,768,384]{2,0,1:T(2,128)}, f32[2,768,384]{2,0,1:T(2,128)})) %all-reduce.8.cloned.1.call-update) | async-done | bytes 7077904
  802.3 127.2 %reduce-scatter.40.cloned.1.call-done = f32[2,48,384]{2,1,0:T(8,128)} async-done(((f32[2,768,384]{2,1,0:T(8,128)}), f32[2,48,384]{2,1,0:T(8,128)}) %reduce-scatter.40.cloned.1.call-update) | async-done | bytes 147472 | tf_op jit(solution)/shard_map/reduce_scatter | solution.py:326
  929.5 177.2 %reduce-scatter.44.cloned.1.call-done = f32[2,48,1536]{2,1,0:T(8,128)} async-done(((f32[2,768,1536]{2,1,0:T(8,128)}), f32[2,48,1536]{2,1,0:T(8,128)}) %reduce-scatter.44.cloned.1.call-update) | async-done | bytes 589840 | tf_op jit(solution)/shard_map/reduce_scatter | solution.py:328
  1106.7 175.9 %reduce-scatter.42.cloned.1.call-done = f32[2,48,1536]{2,1,0:T(8,128)} async-done(((f32[2,768,1536]{2,1,0:T(8,128)}), f32[2,48,1536]{2,1,0:T(8,128)}) %reduce-scatter.42.cloned.1.call-update) | async-done | bytes 589840 | tf_op jit(solution)/shard_map/reduce_scatter | solution.py:327
  (704 shorter events, 400.0 us)
Async XLA Ops:
  7.2 14.9 %all-gather.11.cloned.1.call-start = ((), (), s32[]{:S(2)}) async-start(), calls=%async_computation.15 | async-start | bytes 2359296 | tf_op jit(solution)/shard_map/all_gather | solution.py:116
  7.9 76.6 %reduce-scatter.16.cloned.1.call-start = ((), (), s32[]{:S(2)}) async-start(), calls=%async_computation.16 | async-start | bytes 2359296 | tf_op jit(solution)/shard_map/reduce_scatter | solution.py:122
  65.4 28.1 %reduce-scatter.32.cloned.1.call-start = ((), (), s32[]{:S(2)}) async-start(), calls=%async_computation.30 | async-start | bytes 2359296 | tf_op jit(solution)/shard_map/reduce_scatter | solution.py:122
  83.2 24.9 %all-gather.13.cloned.1.call-start = ((), (), s32[]{:S(2)}) async-start(), calls=%async_computation.17 | async-start | bytes 2359296 | tf_op jit(solution)/shard_map/all_gather | solution.py:129
  83.9 83.8 %copy-start.86 = (f32[768]{0:T(1024)}, f32[768]{0:T(1024)S(1)}, u32[]{:S(2)}) copy-start(f32[768]{0:T(1024)S(1)} %get-tuple-element.490) | copy-start | bytes 9220
  84.5 83.2 %copy-start.94 = (f32[768]{0:T(1024)}, f32[768]{0:T(1024)S(1)}, u32[]{:S(2)}) copy-start(f32[768]{0:T(1024)S(1)} %get-tuple-element.664) | copy-start | bytes 9220
  97.0 30.8 %reduce-scatter.18.cloned.1.call-start = ((), (), s32[]{:S(2)}) async-start(), calls=%async_computation.18 | async-start | bytes 2359296 | tf_op jit(solution)/shard_map/reduce_scatter | solution.py:133
  117.4 26.3 %all-gather.25.cloned.1.call-start = ((), (), s32[]{:S(2)}) async-start(), calls=%async_computation.31 | async-start | bytes 2359296 | tf_op jit(solution)/shard_map/all_gather | solution.py:129
  118.6 49.1 %copy-start.102 = (f32[2,256]{1,0:T(2,128)}, f32[2,256]{1,0:T(2,128)S(1)}, u32[]{:S(2)}) copy-start(f32[2,256]{1,0:T(2,128)S(1)} %broadcast_multiply_fusion.1) | copy-start | bytes 6148
  132.5 35.2 %reduce-scatter.34.cloned.1.call-start = ((), (), s32[]{:S(2)}) async-start(), calls=%async_computation.32 | async-start | bytes 2359296 | tf_op jit(solution)/shard_map/reduce_scatter | solution.py:133
  157.3 26.5 %all-gather.15.cloned.1.call-start = ((), (), s32[]{:S(2)}) async-start(), calls=%async_computation.19 | async-start | bytes 2359296 | tf_op jit(solution)/shard_map/all_gather | solution.py:116
  172.7 68.0 %reduce-scatter.20.cloned.1.call-start = ((), (), s32[]{:S(2)}) async-start(), calls=%async_computation.20 | async-start | bytes 2359296 | tf_op jit(solution)/shard_map/reduce_scatter | solution.py:122
  224.2 26.8 %reduce-scatter.24.cloned.1.call-start = ((), (), s32[]{:S(2)}) async-start(), calls=%async_computation.23 | async-start | bytes 2359296 | tf_op jit(solution)/shard_map/reduce_scatter | solution.py:122
  240.6 25.0 %all-gather.17.cloned.1.call-start = ((), (), s32[]{:S(2)}) async-start(), calls=%async_computation.21 | async-start | bytes 2359296 | tf_op jit(solution)/shard_map/all_gather | solution.py:129
  242.3 126.6 %copy-start.104 = (f32[2,256]{1,0:T(2,128)}, f32[2,256]{1,0:T(2,128)S(1)}, u32[]{:S(2)}) copy-start(f32[2,256]{1,0:T(2,128)S(1)} %broadcast_multiply_fusion.5) | copy-start | bytes 6148
  253.0 115.9 %copy-start.112 = (f32[2,256]{1,0:T(2,128)}, f32[2,256]{1,0:T(2,128)S(1)}, u32[]{:S(2)}) copy-start(f32[2,256]{1,0:T(2,128)S(1)} %add_rsqrt_fusion.1) | copy-start | bytes 6148
  254.4 30.8 %reduce-scatter.22.cloned.1.call-start = ((), (), s32[]{:S(2)}) async-start(), calls=%async_computation.22 | async-start | bytes 2359296 | tf_op jit(solution)/shard_map/reduce_scatter | solution.py:133
  274.9 25.5 %all-gather.19.cloned.1.call-start = ((), (), s32[]{:S(2)}) async-start(), calls=%async_computation.24 | async-start | bytes 2359296 | tf_op jit(solution)/shard_map/all_gather | solution.py:129
  289.2 35.2 %reduce-scatter.26.cloned.1.call-start = ((), (), s32[]{:S(2)}) async-start(), calls=%async_computation.25 | async-start | bytes 2359296 | tf_op jit(solution)/shard_map/reduce_scatter | solution.py:133
  314.1 29.3 %all-gather.21.cloned.1.call-start = ((), (), s32[]{:S(2)}) async-start(), calls=%async_computation.26 | async-start | bytes 2359296 | tf_op jit(solution)/shard_map/all_gather | solution.py:193
  332.2 36.7 %reduce-scatter.28.cloned.1.call-start = ((), (), s32[]{:S(2)}) async-start(), calls=%async_computation.27 | async-start | bytes 2359296 | tf_op jit(solution)/shard_map/reduce_scatter | solution.py:205
  358.5 29.6 %all-gather.23.cloned.1.call-start = ((), (), s32[]{:S(2)}) async-start(), calls=%async_computation.28 | async-start | bytes 2359296 | tf_op jit(solution)/shard_map/all_gather | solution.py:214
  377.0 63.3 %reduce-scatter.30.cloned.1.call-start = ((), (), s32[]{:S(2)}) async-start(), calls=%async_computation.29 | async-start | bytes 2359296 | tf_op jit(solution)/shard_map/reduce_scatter | solution.py:240
  429.9 28.7 %all-gather.27.cloned.1.call-start = ((), (), s32[]{:S(2)}) async-start(), calls=%async_computation.33 | async-start | bytes 2359296 | tf_op jit(solution)/shard_map/all_gather | solution.py:193
  447.4 35.2 %reduce-scatter.36.cloned.1.call-start = ((), (), s32[]{:S(2)}) async-start(), calls=%async_computation.34 | async-start | bytes 2359296 | tf_op jit(solution)/shard_map/reduce_scatter | solution.py:205
  472.2 27.7 %all-gather.29.cloned.1.call-start = ((), (), s32[]{:S(2)}) async-start(), calls=%async_computation.35 | async-start | bytes 2359296 | tf_op jit(solution)/shard_map/all_gather | solution.py:214
  488.7 238.0 %reduce-scatter.38.cloned.1.call-start = ((), (), s32[]{:S(2)}) async-start(), calls=%async_computation.36 | async-start | bytes 2359296 | tf_op jit(solution)/shard_map/reduce_scatter | solution.py:240
  543.5 253.9 %all-reduce.8.cloned.1.call-start = ((), (), s32[]{:S(2)}) async-start(), calls=%async_computation.40 | async-start | bytes 14155776
  566.2 363.3 %reduce-scatter.40.cloned.1.call-start = ((), (), s32[]{:S(2)}) async-start(), calls=%async_computation.37 | async-start | bytes 2506752 | tf_op jit(solution)/shard_map/reduce_scatter | solution.py:326
  572.5 534.2 %reduce-scatter.44.cloned.1.call-start = ((), (), s32[]{:S(2)}) async-start(), calls=%async_computation.39 | async-start | bytes 10027008 | tf_op jit(solution)/shard_map/reduce_scatter | solution.py:328
  586.2 696.3 %reduce-scatter.42.cloned.1.call-start = ((), (), s32[]{:S(2)}) async-start(), calls=%async_computation.38 | async-start | bytes 10027008 | tf_op jit(solution)/shard_map/reduce_scatter | solution.py:327
  605.0 121.7 %copy-start.26 = (f32[2,256,768]{2,1,0:T(8,128)S(1)}, f32[2,256,768]{2,1,0:T(8,128)}, u32[]{:S(2)}) copy-start(f32[2,256,768]{2,1,0:T(8,128)} %copy-done.25) | copy-start | bytes 4718596
  (175 other events, 725.9 us)
Sparse Core Ops, SparseCore 0:
  9.6 12.4 all-gather.10
  65.6 10.2 reduce-scatter.15
  83.3 10.2 reduce-scatter.31
  97.1 10.9 all-gather.12
  117.5 10.2 reduce-scatter.17
  132.6 10.9 all-gather.24
  157.4 10.2 reduce-scatter.33
  172.8 10.9 all-gather.14
  224.3 10.3 reduce-scatter.19
  240.7 10.2 reduce-scatter.23
  254.5 11.0 all-gather.16
  275.0 10.2 reduce-scatter.21
  289.4 10.9 all-gather.18
  314.2 10.2 reduce-scatter.25
  332.3 10.9 all-gather.20
  358.6 10.2 reduce-scatter.27
  377.1 10.9 all-gather.22
  430.0 10.2 reduce-scatter.29
  447.5 10.9 all-gather.26
  472.3 10.1 reduce-scatter.35
  488.8 11.0 all-gather.28
  543.6 10.2 reduce-scatter.37
  566.3 231.1 all-reduce.7
  802.8 126.6 reduce-scatter.39
  936.7 169.9 reduce-scatter.43
  1112.8 169.7 reduce-scatter.41
where the time goes:
time: 1300 us; the launch traced here: 1290 us
  waiting for transfers between devices  741 us (57%)
  matrix products  229 us (18%)
  blocking collectives  120 us (9%)
  local copies, waits for them, and re-layouts  90.8 us (7%)
  other arithmetic  86.7 us (7%)
  between operations  16.8 us (1%)
    reduce_scatter x1, waiting for transfers between devices, shards(): lax.psum_scatter(stacked[11], 'dp', scatter_dimension=1, tiled=True)  177 us
    reduce_scatter x1, waiting for transfers between devices, shards(): lax.psum_scatter(stacked[9], 'dp', scatter_dimension=1, tiled=True)  176 us
    reduce_scatter x1, waiting for transfers between devices, shards(): lax.psum_scatter(stacked[5], 'dp', scatter_dimension=1, tiled=True)  127 us
    psum x1, blocking collectives, shards(): columns = lax.psum((stacked[1], stacked[4], stacked[10]), 'dp')  76.6 us
    unnamed x27, waiting for transfers between devices  69.3 us
    psum x1, blocking collectives, shards(): lax.psum((stacked[6], stacked[7], stacked[8], stacked[12], stacked[13], s...  43.8 us
    all_gather x4, waiting for transfers between devices, forward_layer(): lax.all_gather(normed.astype(jnp.bfloat16), 'mp', axis=1, tiled=True)  43.8 us
    reduce_scatter x4, waiting for transfers between devices, forward_layer(): lax.psum_scatter(partial_down.astype(jnp.bfloat16), 'mp', scatter_dimensi...  38.7 us
  transfers between devices with their start and end apart: 26, of which 23 were waited for; matrix products, arithmetic and copies ran while one was open for 8% of the time, Pallas kernels for 0%

commit v1 on v0

--- a/solution.py
+++ b/solution.py
@@ -329,7 +329,8 @@
     )
     columns = lax.psum((stacked[1], stacked[4], stacked[10]), "dp")
     rows_summed = lax.psum(
-        (stacked[6], stacked[7], stacked[8], stacked[12], stacked[13], stacked[14]), ("dp", "mp")
+        lax.psum((stacked[6], stacked[7], stacked[8], stacked[12], stacked[13], stacked[14]), "dp"),
+        "mp",
     )
     return (
         hidden,

time: 1300 us -> 1300 us (level)
  blocking collectives: 120 us -> 82.8 us
  waiting for transfers between devices: 741 us -> 778 us
    psum x1, blocking collectives: 43.8 us -> 4.03 us  [shards(): lax.psum(lax.psum((stacked[6], stacked[7], stacked[8], stacked[12], stack...]
    unnamed x27, waiting for transfers between devices: 69.3 us -> 106 us
where the time goes in v1:
time: 1300 us; the launch traced here: 1290 us
  waiting for transfers between devices  778 us (60%)
  matrix products  229 us (18%)
  local copies, waits for them, and re-layouts  90.8 us (7%)
  other arithmetic  86.7 us (7%)
  blocking collectives  82.8 us (6%)
  between operations  16.8 us (1%)
    reduce_scatter x1, waiting for transfers between devices, shards(): lax.psum_scatter(stacked[11], 'dp', scatter_dimension=1, tiled=True)  177 us
    reduce_scatter x1, waiting for transfers between devices, shards(): lax.psum_scatter(stacked[9], 'dp', scatter_dimension=1, tiled=True)  176 us
    reduce_scatter x1, waiting for transfers between devices, shards(): lax.psum_scatter(stacked[5], 'dp', scatter_dimension=1, tiled=True)  127 us
    unnamed x27, waiting for transfers between devices  106 us
    psum x1, blocking collectives, shards(): columns = lax.psum((stacked[1], stacked[4], stacked[10]), 'dp')  78.8 us
    all_gather x4, waiting for transfers between devices, forward_layer(): lax.all_gather(normed.astype(jnp.bfloat16), 'mp', axis=1, tiled=True)  43.8 us
    reduce_scatter x4, waiting for transfers between devices, forward_layer(): lax.psum_scatter(partial_down.astype(jnp.bfloat16), 'mp', scatter_dimensi...  38.7 us
    dot_general x8, matrix products, project(): jnp.einsum('rsd,de->rse', left, right, preferred_element_type=jnp.float32)  32.4 us
  transfers between devices with their start and end apart: 26, of which 23 were waited for; matrix products, arithmetic and copies ran while one was open for 8% of the time, Pallas kernels for 0%

profile of v1, /device:TPU:0, one launch (start us, length us, event | category | flops | bytes accessed | tf_op | source)
XLA Modules:
  0.0 1288.9 jit_solution(9016008682052493631)
XLA Ops:
  13.4 8.7 all-gather.11.cloned.1.call-done
  37.4 24.5 %while.72 = (s32[]{:T(128)}, bf16[2,512,384]{1,2,0:T(8,128)(2,1)}, bf16[2,512,384]{1,2,0:T(8,128)(2,1)S(1)}, pred[2,512,512]{1,2,0:T(8,128)(4,1)S(1)}, bf16[2,51...) while((s32[]{:T(128)}, bf16[2,512,384]{1,2,0:T(8,128)(2,1)}, ...), condition=%wide.region_4.5_spmd, body=%wide.region_1.4_spmd.sunk | while | flops 412287488 | bytes 24404124 | solution.py:120
  66.9 11.2 while.76
  97.7 10.5 all-gather.13.cloned.1.call-done
  108.1 9.2 fusion.93
  118.6 9.1 reduce-scatter.18.cloned.1.call-done
  132.6 11.1 all-gather.25.cloned.1.call-done
  158.6 9.1 reduce-scatter.34.cloned.1.call-done
  172.7 11.1 all-gather.15.cloned.1.call-done
  198.1 22.5 %while.73 = (s32[]{:T(128)}, bf16[2,512,384]{1,2,0:T(8,128)(2,1)}, bf16[2,512,384]{1,2,0:T(8,128)(2,1)S(1)}, pred[2,512,512]{1,2,0:T(8,128)(4,1)S(1)}, bf16[2,51...) while((s32[]{:T(128)}, bf16[2,512,384]{1,2,0:T(8,128)(2,1)}, ...), condition=%wide.region_14.15_spmd, body=%wide.region_11.14_spmd.sunk | while | flops 412287488 | bytes 24404124 | solution.py:120
  224.7 11.4 while.74
  242.3 8.7 reduce-scatter.24.cloned.1.call-done
  254.5 11.1 all-gather.17.cloned.1.call-done
  265.6 9.2 fusion.102
  275.1 10.2 reduce-scatter.22.cloned.1.call-done
  289.3 11.1 all-gather.19.cloned.1.call-done
  314.1 10.3 reduce-scatter.26.cloned.1.call-done
  332.3 11.1 all-gather.21.cloned.1.call-done
  358.6 10.3 reduce-scatter.28.cloned.1.call-done
  377.2 10.9 all-gather.23.cloned.1.call-done
  393.5 30.1 %while.75 = (s32[]{:T(128)}, bf16[2,512,384]{1,2,0:T(8,128)(2,1)}, bf16[2,512,384]{1,2,0:T(8,128)(2,1)}, bf16[2,512,384]{1,2,0:T(8,128)(2,1)}, bf16[2,512,384]{1...) while((s32[]{:T(128)}, bf16[2,512,384]{1,2,0:T(8,128)(2,1)}, ...), condition=%wide.region_38.39_spmd, body=%wide.region_36.38_spmd.sunk | while | flops 1031205888 | bytes 93606456 | solution.py:221
  431.6 8.7 reduce-scatter.30.cloned.1.call-done
  447.4 11.1 all-gather.27.cloned.1.call-done
  458.5 8.2 convert_reduce_fusion.1
  472.3 10.3 reduce-scatter.36.cloned.1.call-done
  488.9 11.0 all-gather.29.cloned.1.call-done
  505.1 32.2 %while.77 = (s32[]{:T(128)}, bf16[2,512,384]{1,2,0:T(8,128)(2,1)}, bf16[2,512,384]{1,2,0:T(8,128)(2,1)}, bf16[2,512,384]{1,2,0:T(8,128)(2,1)}, bf16[2,512,384]{1...) while((s32[]{:T(128)}, bf16[2,512,384]{1,2,0:T(8,128)(2,1)}, ...), condition=%wide.region_57.58_spmd, body=%wide.region_55.57_spmd.sunk | while | flops 1031205888 | bytes 87118264 | solution.py:221
  606.4 78.8 %all-reduce.3 = (f32[2,384]{1,0:T(2,128)}, f32[2,384]{1,0:T(2,128)}, f32[2,768]{1,0:T(2,128)S(1)}, f32[2,768]{1,0:T(2,128)S(1)}, f32[2,768]{1,0:T(2,128)S(1)}, /...) all-reduce(f32[2,384]{1,0:T(2,128)S(1)} %pad_maximum_fusion.13, ...), channel_id=1, replica_groups=mesh['dp'=16,'mp'=2] {'dp'}, use_global_device_ids=true, to_apply=%region_62.63 | all-reduce | flops 13824 | bytes 110592 | tf_op jit(solution)/shard_map/psum | solution.py:330
  691.7 105.1 %all-reduce.8.cloned.1.call-done = (f32[2,768,384]{2,0,1:T(2,128)}, f32[2,768,384]{2,0,1:T(2,128)}, f32[2,768,384]{2,0,1:T(2,128)}) async-done(((f32[2,768,384]{2,0,1:T(2,128)}, f32[2,768,384]{2,0,1:T(2,128)}, f32[2,768,384]{2,0,1:T(2,128)}), (f32[2,768,384]{2,0,1:T(2,128)}, f32[2,768,384]{2,0,1:T(2,128)}, f32[2,768,384]{2,0,1:T(2,128)})) %all-reduce.8.cloned.1.call-update) | async-done | bytes 7077904
  801.7 127.2 %reduce-scatter.40.cloned.1.call-done = f32[2,48,384]{2,1,0:T(8,128)} async-done(((f32[2,768,384]{2,1,0:T(8,128)}), f32[2,48,384]{2,1,0:T(8,128)}) %reduce-scatter.40.cloned.1.call-update) | async-done | bytes 147472 | tf_op jit(solution)/shard_map/reduce_scatter | solution.py:326
  928.9 177.2 %reduce-scatter.44.cloned.1.call-done = f32[2,48,1536]{2,1,0:T(8,128)} async-done(((f32[2,768,1536]{2,1,0:T(8,128)}), f32[2,48,1536]{2,1,0:T(8,128)}) %reduce-scatter.44.cloned.1.call-update) | async-done | bytes 589840 | tf_op jit(solution)/shard_map/reduce_scatter | solution.py:328
  1106.1 175.9 %reduce-scatter.42.cloned.1.call-done = f32[2,48,1536]{2,1,0:T(8,128)} async-done(((f32[2,768,1536]{2,1,0:T(8,128)}), f32[2,48,1536]{2,1,0:T(8,128)}) %reduce-scatter.42.cloned.1.call-update) | async-done | bytes 589840 | tf_op jit(solution)/shard_map/reduce_scatter | solution.py:327
  (704 shorter events, 395.9 us)
Async XLA Ops:
  7.2 14.9 %all-gather.11.cloned.1.call-start = ((), (), s32[]{:S(2)}) async-start(), calls=%async_computation.15 | async-start | bytes 2359296 | tf_op jit(solution)/shard_map/all_gather | solution.py:116
  7.9 76.6 %reduce-scatter.16.cloned.1.call-start = ((), (), s32[]{:S(2)}) async-start(), calls=%async_computation.16 | async-start | bytes 2359296 | tf_op jit(solution)/shard_map/reduce_scatter | solution.py:122
  65.4 28.1 %reduce-scatter.32.cloned.1.call-start = ((), (), s32[]{:S(2)}) async-start(), calls=%async_computation.30 | async-start | bytes 2359296 | tf_op jit(solution)/shard_map/reduce_scatter | solution.py:122
  83.2 24.9 %all-gather.13.cloned.1.call-start = ((), (), s32[]{:S(2)}) async-start(), calls=%async_computation.17 | async-start | bytes 2359296 | tf_op jit(solution)/shard_map/all_gather | solution.py:129
  83.9 83.8 %copy-start.86 = (f32[768]{0:T(1024)}, f32[768]{0:T(1024)S(1)}, u32[]{:S(2)}) copy-start(f32[768]{0:T(1024)S(1)} %get-tuple-element.490) | copy-start | bytes 9220
  84.5 83.2 %copy-start.94 = (f32[768]{0:T(1024)}, f32[768]{0:T(1024)S(1)}, u32[]{:S(2)}) copy-start(f32[768]{0:T(1024)S(1)} %get-tuple-element.670) | copy-start | bytes 9220
  97.0 30.8 %reduce-scatter.18.cloned.1.call-start = ((), (), s32[]{:S(2)}) async-start(), calls=%async_computation.18 | async-start | bytes 2359296 | tf_op jit(solution)/shard_map/reduce_scatter | solution.py:133
  117.4 26.3 %all-gather.25.cloned.1.call-start = ((), (), s32[]{:S(2)}) async-start(), calls=%async_computation.31 | async-start | bytes 2359296 | tf_op jit(solution)/shard_map/all_gather | solution.py:129
  118.6 49.1 %copy-start.102 = (f32[2,256]{1,0:T(2,128)}, f32[2,256]{1,0:T(2,128)S(1)}, u32[]{:S(2)}) copy-start(f32[2,256]{1,0:T(2,128)S(1)} %broadcast_multiply_fusion.1) | copy-start | bytes 6148
  132.5 35.2 %reduce-scatter.34.cloned.1.call-start = ((), (), s32[]{:S(2)}) async-start(), calls=%async_computation.32 | async-start | bytes 2359296 | tf_op jit(solution)/shard_map/reduce_scatter | solution.py:133
  157.3 26.5 %all-gather.15.cloned.1.call-start = ((), (), s32[]{:S(2)}) async-start(), calls=%async_computation.19 | async-start | bytes 2359296 | tf_op jit(solution)/shard_map/all_gather | solution.py:116
  172.7 68.0 %reduce-scatter.20.cloned.1.call-start = ((), (), s32[]{:S(2)}) async-start(), calls=%async_computation.20 | async-start | bytes 2359296 | tf_op jit(solution)/shard_map/reduce_scatter | solution.py:122
  224.2 26.8 %reduce-scatter.24.cloned.1.call-start = ((), (), s32[]{:S(2)}) async-start(), calls=%async_computation.23 | async-start | bytes 2359296 | tf_op jit(solution)/shard_map/reduce_scatter | solution.py:122
  240.6 25.0 %all-gather.17.cloned.1.call-start = ((), (), s32[]{:S(2)}) async-start(), calls=%async_computation.21 | async-start | bytes 2359296 | tf_op jit(solution)/shard_map/all_gather | solution.py:129
  242.3 126.6 %copy-start.104 = (f32[2,256]{1,0:T(2,128)}, f32[2,256]{1,0:T(2,128)S(1)}, u32[]{:S(2)}) copy-start(f32[2,256]{1,0:T(2,128)S(1)} %broadcast_multiply_fusion.5) | copy-start | bytes 6148
  253.0 115.9 %copy-start.112 = (f32[2,256]{1,0:T(2,128)}, f32[2,256]{1,0:T(2,128)S(1)}, u32[]{:S(2)}) copy-start(f32[2,256]{1,0:T(2,128)S(1)} %add_rsqrt_fusion.1) | copy-start | bytes 6148
  254.4 30.8 %reduce-scatter.22.cloned.1.call-start = ((), (), s32[]{:S(2)}) async-start(), calls=%async_computation.22 | async-start | bytes 2359296 | tf_op jit(solution)/shard_map/reduce_scatter | solution.py:133
  274.9 25.5 %all-gather.19.cloned.1.call-start = ((), (), s32[]{:S(2)}) async-start(), calls=%async_computation.24 | async-start | bytes 2359296 | tf_op jit(solution)/shard_map/all_gather | solution.py:129
  289.2 35.2 %reduce-scatter.26.cloned.1.call-start = ((), (), s32[]{:S(2)}) async-start(), calls=%async_computation.25 | async-start | bytes 2359296 | tf_op jit(solution)/shard_map/reduce_scatter | solution.py:133
  314.1 29.3 %all-gather.21.cloned.1.call-start = ((), (), s32[]{:S(2)}) async-start(), calls=%async_computation.26 | async-start | bytes 2359296 | tf_op jit(solution)/shard_map/all_gather | solution.py:193
  332.2 36.7 %reduce-scatter.28.cloned.1.call-start = ((), (), s32[]{:S(2)}) async-start(), calls=%async_computation.27 | async-start | bytes 2359296 | tf_op jit(solution)/shard_map/reduce_scatter | solution.py:205
  358.5 29.6 %all-gather.23.cloned.1.call-start = ((), (), s32[]{:S(2)}) async-start(), calls=%async_computation.28 | async-start | bytes 2359296 | tf_op jit(solution)/shard_map/all_gather | solution.py:214
  377.0 63.3 %reduce-scatter.30.cloned.1.call-start = ((), (), s32[]{:S(2)}) async-start(), calls=%async_computation.29 | async-start | bytes 2359296 | tf_op jit(solution)/shard_map/reduce_scatter | solution.py:240
  429.9 28.7 %all-gather.27.cloned.1.call-start = ((), (), s32[]{:S(2)}) async-start(), calls=%async_computation.33 | async-start | bytes 2359296 | tf_op jit(solution)/shard_map/all_gather | solution.py:193
  447.4 35.2 %reduce-scatter.36.cloned.1.call-start = ((), (), s32[]{:S(2)}) async-start(), calls=%async_computation.34 | async-start | bytes 2359296 | tf_op jit(solution)/shard_map/reduce_scatter | solution.py:205
  472.2 27.7 %all-gather.29.cloned.1.call-start = ((), (), s32[]{:S(2)}) async-start(), calls=%async_computation.35 | async-start | bytes 2359296 | tf_op jit(solution)/shard_map/all_gather | solution.py:214
  488.7 200.5 %reduce-scatter.38.cloned.1.call-start = ((), (), s32[]{:S(2)}) async-start(), calls=%async_computation.36 | async-start | bytes 2359296 | tf_op jit(solution)/shard_map/reduce_scatter | solution.py:240
  543.5 253.3 %all-reduce.8.cloned.1.call-start = ((), (), s32[]{:S(2)}) async-start(), calls=%async_computation.40 | async-start | bytes 14155776
  566.2 362.7 %reduce-scatter.40.cloned.1.call-start = ((), (), s32[]{:S(2)}) async-start(), calls=%async_computation.37 | async-start | bytes 2506752 | tf_op jit(solution)/shard_map/reduce_scatter | solution.py:326
  572.5 533.6 %reduce-scatter.44.cloned.1.call-start = ((), (), s32[]{:S(2)}) async-start(), calls=%async_computation.39 | async-start | bytes 10027008 | tf_op jit(solution)/shard_map/reduce_scatter | solution.py:328
  586.2 695.7 %reduce-scatter.42.cloned.1.call-start = ((), (), s32[]{:S(2)}) async-start(), calls=%async_computation.38 | async-start | bytes 10027008 | tf_op jit(solution)/shard_map/reduce_scatter | solution.py:327
  605.0 84.1 %copy-start.26 = (f32[2,256,768]{2,1,0:T(8,128)S(1)}, f32[2,256,768]{2,1,0:T(8,128)}, u32[]{:S(2)}) copy-start(f32[2,256,768]{2,1,0:T(8,128)} %copy-done.25) | copy-start | bytes 4718596
  (175 other events, 704.7 us)
Sparse Core Ops, SparseCore 0:
  9.6 12.4 all-gather.10
  65.6 10.2 reduce-scatter.15
  83.3 10.2 reduce-scatter.31
  97.1 10.9 all-gather.12
  117.5 10.2 reduce-scatter.17
  132.6 10.9 all-gather.24
  157.4 10.2 reduce-scatter.33
  172.8 10.9 all-gather.14
  224.3 10.3 reduce-scatter.19
  240.7 10.2 reduce-scatter.23
  254.5 11.0 all-gather.16
  275.0 10.2 reduce-scatter.21
  289.4 10.9 all-gather.18
  314.2 10.2 reduce-scatter.25
  332.3 10.9 all-gather.20
  358.6 10.2 reduce-scatter.27
  377.1 10.9 all-gather.22
  430.0 10.2 reduce-scatter.29
  447.5 10.9 all-gather.26
  472.3 10.1 reduce-scatter.35
  488.8 11.0 all-gather.28
  543.6 10.2 reduce-scatter.37
  566.3 230.4 all-reduce.7
  802.1 126.6 reduce-scatter.39
  936.1 169.9 reduce-scatter.43
  1112.2 169.7 reduce-scatter.41
